TPU v7x, 256 devices: a whole 4x4x8 slice. The times are simulated.
256 devices in a mesh: leaf: 128 (over y, x, z), sub: 2 (over core).
Axes of the slice: x: 4, y: 4, z: 8, core: 2. Of those that a mesh axis runs over, the one named last changes fastest.
Arguments:
- density: bfloat16 [1024, 256, 32], P('leaf', None, 'sub'), may hold values from -6 to 6
- near_blocks: bfloat16 [1024, 6, 256, 256], P('leaf', 'sub'), may hold values from -0.15625 to 0.15625
- near_index: int32 [1024, 6], P('leaf', 'sub'), may hold values from 0 to 1023, as said below
- col_basis: bfloat16 [1024, 256, 64], P('leaf'), may hold values from -0.375 to 0.375
- row_basis: bfloat16 [1024, 256, 64], P('leaf'), may hold values from -0.75 to 0.75
- leaf_coupling: bfloat16 [1024, 6, 64, 64], P('leaf', 'sub'), may hold values from -0.3125 to 0.3125
- leaf_list: int32 [1024, 6], P('leaf', 'sub'), may hold values from 0 to 1023, as said below
- leaf_up: bfloat16 [1024, 64, 64], P('leaf'), may hold values from -0.25 to 0.25
- leaf_down: bfloat16 [1024, 64, 64], P('leaf'), may hold values from -0.75 to 0.75
- node_coupling: bfloat16 [128, 4, 64, 64], P('leaf'), may hold values from -0.375 to 0.375
- node_list: int32 [128, 4], P('leaf'), may hold values from 0 to 127, as said below
- node_up: bfloat16 [128, 64, 64], P('leaf'), may hold values from -0.5 to 0.5
- node_down: bfloat16 [128, 64, 64], P('leaf'), may hold values from -0.75 to 0.75
- upper_coupling: bfloat16 [126, 4, 64, 64], replicated, may hold values from -0.375 to 0.375
- upper_list: int32 [126, 4], replicated, may hold values from 2 to 127, as said below
- upper_up: bfloat16 [124, 64, 64], replicated, may hold values from -0.5 to 0.5
- upper_down: bfloat16 [124, 64, 64], replicated, may hold values from -0.75 to 0.75
Outputs:
- potential: bfloat16 [1024, 256, 32], P('leaf', None, 'sub')
Inputs may be any that keep to these rules, and one draw needn't show every extreme that they name: `near_index`: row t holds 6 different leaves, the first being t itself; all lie among the leaves of t's own block of 8 and of the blocks just before and after it; none stands in row t of leaf_list. `leaf_list`: row t holds 6 different leaves other than t, all among the leaves of t's own block of 8 and of the blocks just before and after it. `node_list`: row d holds 4 different clusters other than d; the first is (d + 64) mod 128. `upper_list`: row n - 2 names nodes of node n's level other than n, possibly repeated; the first is the node half that level's size away.
All inputs are finite; a program needn't handle non-finite values.
Results may differ from a plain program's by a relative error of at most 0.029.
Values may be sent and summed in bfloat16 or wider, within the bound.
A program may use at most 128 MiB of HBM per device.

v0:
```python
import jax
import jax.numpy as jnp
from jax import lax
from jax.sharding import PartitionSpec as P


def extended_2(block, sides, width):
    for axis, dim in sides:
        count = lax.axis_size(axis)
        forward = [(i, i + 1) for i in range(count - 1)]
        backward = [(target, source) for source, target in forward]
        low = lax.ppermute(
            lax.slice_in_dim(block, block.shape[dim] - width, None, axis=dim), axis, forward
        )
        high = lax.ppermute(lax.slice_in_dim(block, 0, width, axis=dim), axis, backward)
        block = jnp.concatenate([low, block, high], axis=dim)
    return block


def upper_tree(raised_coefficients, upper_coupling, upper_list, upper_up, upper_down, node_count):
    levels = node_count.bit_length() - 1
    rank_size = raised_coefficients.shape[1]
    columns = raised_coefficients.shape[2]
    coeffs = {}
    summed = (
        raised_coefficients.astype(jnp.float32)
        .reshape(node_count // 2, 2, rank_size, columns)
        .sum(axis=1)
    )
    coeffs[levels - 1] = summed.astype(jnp.bfloat16)
    for height in range(levels - 2, 0, -1):
        lower_size = 2 ** (height + 1)
        matrices = upper_up[lower_size - 4 : 2 * lower_size - 4]
        shifted = jnp.einsum(
            "nrs,nrc->nsc", matrices, coeffs[height + 1], preferred_element_type=jnp.float32
        )
        coeffs[height] = (
            shifted.reshape(lower_size // 2, 2, rank_size, columns).sum(axis=1).astype(jnp.bfloat16)
        )
    answer = None
    for height in range(1, levels):
        breadth = 2**height
        listed = upper_list[breadth - 2 : 2 * breadth - 2] - breadth
        sources = coeffs[height][listed]
        coupled = jnp.einsum(
            "nfrs,nfsc->nrc",
            upper_coupling[breadth - 2 : 2 * breadth - 2],
            sources,
            preferred_element_type=jnp.float32,
        )
        if height > 1:
            parents = jnp.repeat(answer, 2, axis=0)
            coupled = coupled + jnp.einsum(
                "nrs,nsc->nrc",
                upper_down[breadth - 4 : 2 * breadth - 4],
                parents,
                preferred_element_type=jnp.float32,
            )
        answer = coupled.astype(jnp.bfloat16)
    return answer


def body(
    density,
    near_blocks,
    near_index,
    col_basis,
    row_basis,
    leaf_coupling,
    leaf_list,
    leaf_up,
    leaf_down,
    node_coupling,
    node_list,
    node_up,
    node_down,
    upper_coupling,
    upper_list,
    upper_up,
    upper_down,
):
    leaf_count = density.shape[0]
    half_cols = density.shape[2]
    device = lax.axis_index("leaf")
    core_index = lax.axis_index("sub")
    node_count = lax.axis_size("leaf")
    charge_input = lax.all_gather(density, "sub", axis=2, tiled=True)
    block_entries, couplings = (near_blocks, leaf_coupling)
    near_cols, far_cols = (near_index, leaf_list)
    extended = extended_2(charge_input, (("leaf", 0),), leaf_count)
    offset = device * leaf_count - leaf_count
    leaf_coeff = jnp.einsum(
        "tlr,tlc->trc", col_basis, charge_input, preferred_element_type=jnp.float32
    ).astype(jnp.bfloat16)
    coeff_ext = extended_2(leaf_coeff, (("leaf", 0),), leaf_count)
    selected_nodes = extended[near_cols - offset]
    proximate_portion = jnp.einsum(
        "vpqx,vpxn->vqn", block_entries, selected_nodes, preferred_element_type=jnp.float32
    )
    far_sources = coeff_ext[far_cols - offset]
    far_part = jnp.einsum(
        "tjrs,tjsc->trc", couplings, far_sources, preferred_element_type=jnp.float32
    )
    proximate_field, far_field = (
        lax.psum_scatter(
            proximate_portion.astype(jnp.bfloat16), "sub", scatter_dimension=2, tiled=True
        ).astype(jnp.float32),
        lax.psum_scatter(
            far_part.astype(jnp.bfloat16), "sub", scatter_dimension=2, tiled=True
        ).astype(jnp.float32),
    )
    own_coeff = lax.dynamic_slice_in_dim(leaf_coeff, core_index * half_cols, half_cols, 2)
    node_coeff = jnp.einsum(
        "trs,trc->sc", leaf_up, own_coeff, preferred_element_type=jnp.float32
    ).astype(jnp.bfloat16)
    raised_coefficients = jnp.einsum(
        "rs,rc->sc", node_up[0], node_coeff, preferred_element_type=jnp.float32
    ).astype(jnp.bfloat16)
    all_coeff, all_lifted = (
        lax.all_gather(node_coeff[None], "leaf", axis=0, tiled=True),
        lax.all_gather(raised_coefficients[None], "leaf", axis=0, tiled=True),
    )
    answer = upper_tree(all_lifted, upper_coupling, upper_list, upper_up, upper_down, node_count)
    parent_field = lax.dynamic_index_in_dim(answer, device // 2, 0, keepdims=False)
    node_term = jnp.einsum(
        "frs,fsc->rc", node_coupling[0], all_coeff[node_list[0]], preferred_element_type=jnp.float32
    )
    node_term = node_term + jnp.dot(node_down[0], parent_field, preferred_element_type=jnp.float32)
    node_field = node_term.astype(jnp.bfloat16)
    descended = jnp.einsum("trs,sc->trc", leaf_down, node_field, preferred_element_type=jnp.float32)
    leaf_field = (far_field + descended).astype(jnp.bfloat16)
    farther = jnp.einsum("tlr,trc->tlc", row_basis, leaf_field, preferred_element_type=jnp.float32)
    return (proximate_field + farther).astype(jnp.bfloat16)


def solution(mesh):
    placed = (
        P("leaf", None, "sub"),
        P("leaf", "sub", None, None),
        P("leaf", "sub"),
        P("leaf", None, None),
        P("leaf", None, None),
        P("leaf", "sub", None, None),
        P("leaf", "sub"),
        P("leaf", None, None),
        P("leaf", None, None),
        P("leaf", None, None, None),
        P("leaf", None),
        P("leaf", None, None),
        P("leaf", None, None),
        P(),
        P(),
        P(),
        P(),
    )
    return jax.shard_map(
        body, mesh=mesh, in_specs=placed, out_specs=P("leaf", None, "sub"), check_vma=False
    )
```

profile of v0, /device:TPU:1, one launch (start us, length us, event | category | flops | bytes accessed | tf_op | source)
XLA Modules:
  0.0 899.4 jit_solution(17563113812519195324)
XLA Ops:
  6.5 6.9 all_gather.9
  16.6 4.6 collective-permute-start.2
  22.5 4.6 collective-permute-start
  31.7 2.7 slice.77
  34.3 2.6 slice.74
  45.3 3.2 slice.79
  48.5 3.2 slice.76
  51.7 3.2 slice.73
  54.9 3.2 slice.70
  58.2 3.2 slice.67
  66.3 2.4 copy.108
  68.7 2.4 copy.106
  71.0 4.7 copy.107
  76.8 292.5 %all-gather.3 = bf16[128,64,16]{1,2,0:T(8,128)(2,1)S(1)} all-gather(bf16[1,64,16]{1,2,0:T(8,128)(2,1)S(1)} %fusion.21), channel_id=3, replica_groups=mesh['leaf'=128,'sub'=2] {'leaf'}, dimensions={0}, use_global_device_ids=true | all-gather | bytes 264192 | tf_op jit(solution)/shard_map/all_gather | solution.py:121
  369.4 305.1 %all-gather.2 = bf16[128,64,16]{1,2,0:T(8,128)(2,1)} all-gather(bf16[1,64,16]{1,2,0:T(8,128)(2,1)S(1)} %bitcast.201), channel_id=2, replica_groups=mesh['leaf'=128,'sub'=2] {'leaf'}, dimensions={0}, use_global_device_ids=true | all-gather | bytes 264192 | tf_op jit(solution)/shard_map/all_gather | solution.py:120
  674.5 2.3 copy.104
  676.8 2.4 copy.102
  679.2 2.8 copy.100
  682.1 3.3 copy.98
  698.7 2.8 copy.111
  701.4 2.5 copy.110
  703.9 2.3 copy.109
  706.2 3.3 copy.112
  709.5 4.9 copy.105
  714.4 4.7 copy.103
  719.0 5.0 copy.101
  724.0 6.1 copy.99
  730.1 7.2 copy.97
  745.9 2.7 convolution_bitcast_fusion.1
  759.0 2.7 fusion.5
  766.5 107.6 %reduce-scatter.5.cloned.1.call-done = bf16[8,64,16]{1,2,0:T(8,128)(2,1)} async-done(((bf16[8,64,32]{1,2,0:T(8,128)(2,1)}), bf16[8,64,16]{1,2,0:T(8,128)(2,1)}) %reduce-scatter.5.cloned.1.call-update) | async-done | bytes 16400 | tf_op jit(solution)/shard_map/reduce_scatter | solution.py:108
  874.1 16.6 %reduce-scatter.3.cloned.1.call-done = bf16[8,256,16]{1,2,0:T(8,128)(2,1)} async-done(((bf16[8,256,32]{1,2,0:T(8,128)(2,1)}), bf16[8,256,16]{1,2,0:T(8,128)(2,1)}) %reduce-scatter.3.cloned.1.call-update) | async-done | bytes 65552 | tf_op jit(solution)/shard_map/reduce_scatter | solution.py:105
  (128 shorter events, 62.1 us)
Async XLA Ops:
  6.5 752.4 %copy-start = (bf16[8,3,256,256]{3,2,1,0:T(8,128)(2,1)S(1)}, bf16[8,3,256,256]{3,2,1,0:T(8,128)(2,1)}, u32[]{:S(2)}) copy-start(bf16[8,3,256,256]{3,2,1,0:T(8,128)(2,1)} %param.18) | copy-start | bytes 9437188
  6.5 867.6 %reduce-scatter.5.cloned.1.call-start = ((), (), s32[]{:S(2)}) async-start(), calls=%async_computation.3 | async-start | bytes 98304 | tf_op jit(solution)/shard_map/reduce_scatter | solution.py:108
  15.3 737.7 %collective-permute-start.3 = (bf16[8,64,32]{1,2,0:T(8,128)(2,1)}, bf16[8,64,32]{1,2,0:T(8,128)(2,1)}, u32[]{:S(2)}, u32[]{:S(2)}) collective-permute-start(bf16[8,64,32]{1,2,0:T(8,128)(2,1)} %convolution_convert_fusion), channel_id=1, source_target_pairs={{2,0},{4,2},{6,4},{8,6},{10,8},{12,10},{14,12},{16,14},{18,16},{20... | collective-permute-start | bytes 98312 | tf_op jit(solution)/shard_map/ppermute | solution.py:15
  16.6 736.4 %collective-permute-start.2 = (bf16[8,64,32]{1,2,0:T(8,128)(2,1)}, bf16[8,64,32]{1,2,0:T(8,128)(2,1)}, u32[]{:S(2)}, u32[]{:S(2)}) collective-permute-start(bf16[8,64,32]{1,2,0:T(8,128)(2,1)} %convolution_convert_fusion), channel_id=1, source_target_pairs={{0,2},{2,4},{4,6},{6,8},{8,10},{10,12},{12,14},{14,16},{16,18},{18... | collective-permute-start | bytes 98312 | tf_op jit(solution)/shard_map/ppermute | solution.py:12
  21.2 735.3 %collective-permute-start.1 = (bf16[8,256,32]{1,2,0:T(8,128)(2,1)}, bf16[8,256,32]{1,2,0:T(8,128)(2,1)}, u32[]{:S(2)}, u32[]{:S(2)}) collective-permute-start(bf16[8,256,32]{1,2,0:T(8,128)(2,1)} %all_gather.9), channel_id=1, source_target_pairs={{2,0},{4,2},{6,4},{8,6},{10,8},{12,10},{14,12},{16,14},{18,16},{20... | collective-permute-start | bytes 393224 | tf_op jit(solution)/shard_map/ppermute | solution.py:15
  22.5 734.0 %collective-permute-start = (bf16[8,256,32]{1,2,0:T(8,128)(2,1)}, bf16[8,256,32]{1,2,0:T(8,128)(2,1)}, u32[]{:S(2)}, u32[]{:S(2)}) collective-permute-start(bf16[8,256,32]{1,2,0:T(8,128)(2,1)} %all_gather.9), channel_id=1, source_target_pairs={{0,2},{2,4},{4,6},{6,8},{8,10},{10,12},{12,14},{14,16},{16,18},{18... | collective-permute-start | bytes 393224 | tf_op jit(solution)/shard_map/ppermute | solution.py:12
  27.1 9.8 %copy-start.3 = (bf16[124,64,64]{0,2,1:T(8,128)(2,1)S(1)}, bf16[124,64,64]{0,2,1:T(8,128)(2,1)}, u32[]{:S(2)}) copy-start(bf16[124,64,64]{0,2,1:T(8,128)(2,1)} %param.32) | copy-start | bytes 3047428
  31.7 8.0 copy-start.2
  39.7 5.7 copy-start.1
  58.2 3.2 copy-start.19
  58.2 6.0 copy-start.16
  58.2 6.0 copy-start.17
  61.4 14.4 %copy-start.13 = (bf16[8,64,64]{2,1,0:T(8,128)(2,1)S(1)}, bf16[8,64,64]{2,1,0:T(8,128)(2,1)}, u32[]{:S(2)}) copy-start(bf16[8,64,64]{2,1,0:T(8,128)(2,1)} %param.24) | copy-start | bytes 196612
  61.4 15.4 %copy-start.15 = (bf16[1,64,64]{2,1,0:T(8,128)(2,1)S(1)}, bf16[1,64,64]{2,1,0:T(8,128)(2,1)}, u32[]{:S(2)}) copy-start(bf16[1,64,64]{2,1,0:T(8,128)(2,1)} %param.28) | copy-start | bytes 24580
  730.1 11.0 %copy-start.9 = (bf16[32,64,16]{1,2,0:T(8,128)(2,1)S(1)}, bf16[32,64,16]{1,2,0:T(8,128)(2,1)}, u32[]{:S(2)}) copy-start(bf16[32,64,16]{1,2,0:T(8,128)(2,1)} %gather_fusion.6) | copy-start | bytes 196612
  737.4 11.2 %copy-start.6 = (bf16[64,64,16]{1,2,0:T(8,128)(2,1)S(1)}, bf16[64,64,16]{1,2,0:T(8,128)(2,1)}, u32[]{:S(2)}) copy-start(bf16[64,64,16]{1,2,0:T(8,128)(2,1)} %gather_fusion.5) | copy-start | bytes 393220
  738.8 9.8 %copy-start.7 = (bf16[16,4,64,64]{3,2,1,0:T(8,128)(2,1)S(1)}, bf16[16,4,64,64]{3,2,1,0:T(8,128)(2,1)}, u32[]{:S(2)}) copy-start(bf16[16,4,64,64]{3,2,1,0:T(8,128)(2,1)} %copy.101) | copy-start | bytes 1572868
  738.8 10.3 %copy-start.10 = (bf16[32,64,64]{2,1,0:T(8,128)(2,1)S(1)}, bf16[32,64,64]{2,1,0:T(8,128)(2,1)}, u32[]{:S(2)}) copy-start(bf16[32,64,64]{2,1,0:T(8,128)(2,1)} %copy.111) | copy-start | bytes 786436
  738.8 10.7 %copy-start.8 = (bf16[64,64,64]{2,1,0:T(8,128)(2,1)S(1)}, bf16[64,64,64]{2,1,0:T(8,128)(2,1)}, u32[]{:S(2)}) copy-start(bf16[64,64,64]{2,1,0:T(8,128)(2,1)} %copy.112) | copy-start | bytes 1572868
  744.5 6.4 copy-start.4
  744.6 6.4 copy-start.5
  749.4 3.5 copy-start.18
  749.4 4.5 copy-start.14
  756.4 134.3 %reduce-scatter.3.cloned.1.call-start = ((), (), s32[]{:S(2)}) async-start(), calls=%async_computation.2 | async-start | bytes 196608 | tf_op jit(solution)/shard_map/reduce_scatter | solution.py:105
  758.9 131.8 %copy-start.11 = (bf16[8,256,64]{1,2,0:T(8,128)(2,1)S(1)}, bf16[8,256,64]{1,2,0:T(8,128)(2,1)}, u32[]{:S(2)}) copy-start(bf16[8,256,64]{1,2,0:T(8,128)(2,1)} %param.21) | copy-start | bytes 786436
  759.0 131.8 %copy-start.12 = (bf16[8,64,64]{2,1,0:T(8,128)(2,1)S(1)}, bf16[8,64,64]{2,1,0:T(8,128)(2,1)}, u32[]{:S(2)}) copy-start(bf16[8,64,64]{2,1,0:T(8,128)(2,1)} %param.25) | copy-start | bytes 196612
Sparse Core Ops, SparseCore 0:
  756.6 117.5 reduce-scatter.4
  876.6 14.0 reduce-scatter.2
where the time goes:
time: 901 us; the launch traced here: 899 us
  blocking collectives  604 us (67%)
  waiting for transfers between devices  124 us (14%)
  local copies, waits for them, and re-layouts  103 us (11%)
  matrix products  31.2 us (3%)
  between operations  13.7 us (2%)
  starting transfers between devices  11.9 us (1%)
  other arithmetic  10.8 us (1%)
    all_gather x1, blocking collectives, body(): lax.all_gather(node_coeff[None], 'leaf', axis=0, tiled=True)  305 us
    all_gather x1, blocking collectives, body(): lax.all_gather(raised_coefficients[None], 'leaf', axis=0, tiled=True)  292 us
    reduce_scatter x1, waiting for transfers between devices, body(): lax.psum_scatter(far_part.astype(jnp.bfloat16), 'sub', scatter_dimension=...  108 us
    unnamed x56, local copies, waits for them, and re-layouts  59 us
  transfers between devices with their start and end apart: 6, of which 2 were waited for; matrix products, arithmetic and copies ran while one was open for 16% of the time, Pallas kernels for 0%

commit v1 on v0

v1 whole, which is shorter than its diff:
```python
import jax
import jax.numpy as jnp
from jax import lax
from jax.experimental import pallas as pl
from jax.experimental.pallas import tpu as pltpu
from jax.sharding import PartitionSpec as P

MESH = pl.DeviceIdType.MESH
F32 = jnp.float32
BF16 = jnp.bfloat16

LEAVES = 8
COLS = 16
RANK = 64
RING = 8
PLANE = 16
DEVS = RING * PLANE
TILES = 9


def dot(a, b):
    return jnp.dot(a, b, preferred_element_type=F32)


def dot_nt(a, b):
    return lax.dot_general(a, b, (((1,), (1,)), ((), ())), preferred_element_type=F32)


def within(i, first, last):
    return jnp.minimum(jnp.maximum(i, first), last)


def kernel(
    dens_hbm,
    near_hbm,
    near_idx,
    colb_hbm,
    rowb_hbm,
    lcoup_hbm,
    leaf_idx,
    lup_hbm,
    ldown_hbm,
    ncoup_hbm,
    node_idx,
    nup_hbm,
    ndown_hbm,
    upc_hbm,
    upper_idx,
    upu_hbm,
    upd_hbm,
    out_ref,
    dens_win,
    near_v,
    colb_v,
    rowb_v,
    lcoup_v,
    lup_v,
    ldown_v,
    ncoup_v,
    nup_v,
    ndown_v,
    upc_v,
    upu_v,
    upd_v,
    lc_win,
    zbuf,
    tab,
    sel_up,
    sel_c,
    sel_d,
    near_own,
    near_out,
    near_in,
    far_own,
    far_out,
    far_in,
    load_sem,
    z_send,
    z_recv,
    p_send,
    p_recv,
    d_send,
    d_recv,
    l_send,
    l_recv,
    x_send,
    x_recv,
):
    leaf = lax.axis_index("leaf")
    sub = lax.axis_index("sub")
    other = 1 - sub
    group = leaf // RING
    z = leaf % RING
    mid = pl.ds(LEAVES, LEAVES)

    loads = [
        (dens_hbm, dens_win.at[mid, pl.ds(0, COLS), :]),
        (colb_hbm, colb_v),
        (lup_hbm, lup_v),
        (nup_hbm, nup_v),
        (upu_hbm, upu_v),
        (upc_hbm, upc_v),
        (near_hbm, near_v),
        (lcoup_hbm, lcoup_v),
        (upd_hbm, upd_v),
        (ndown_hbm, ndown_v),
        (ncoup_hbm, ncoup_v),
        (ldown_hbm, ldown_v),
        (rowb_hbm, rowb_v),
    ]
    load = [
        pltpu.make_async_copy(src, dst, load_sem.at[i]) for i, (src, dst) in enumerate(loads)
    ]
    for copy in load:
        copy.start()

    def ring_peer(k):
        return {"leaf": group * RING + (z + k) % RING, "sub": sub}

    def plane_peer(k):
        return {"leaf": ((group + k) % PLANE) * RING + z, "sub": sub}

    after, before = (leaf + 1) % DEVS, (leaf + DEVS - 1) % DEVS
    neighbours = [
        ({"leaf": leaf, "sub": other}, LEAVES, COLS),
        ({"leaf": after, "sub": sub}, 0, 0),
        ({"leaf": after, "sub": other}, 0, COLS),
        ({"leaf": before, "sub": sub}, 2 * LEAVES, 0),
        ({"leaf": before, "sub": other}, 2 * LEAVES, COLS),
    ]

    barrier = pltpu.get_barrier_semaphore()
    greeted = (
        [ring_peer(k) for k in range(1, RING)]
        + [plane_peer(k) for k in range(1, PLANE)]
        + [device for device, _, _ in neighbours]
    )
    for device in greeted:
        pl.semaphore_signal(barrier, inc=1, device_id=device, device_id_type=MESH)

    load[0].wait()
    load[1].wait()
    pairs = []
    for i in range(LEAVES // 2):
        halves = [
            dot_nt(dens_win[LEAVES + t, 0:COLS, :], colb_v[t]) for t in (2 * i, 2 * i + 1)
        ]
        pair = jnp.concatenate(halves, axis=1).astype(BF16)
        lc_win[LEAVES // 2 + i, 0:COLS, :] = pair
        pairs.append(pair)
    load[2].wait()
    load[3].wait()
    raw = dot(jnp.concatenate(pairs, axis=1), lup_v[...].reshape(LEAVES * RANK, RANK))
    raised = dot(raw.astype(BF16), nup_v[0])
    zbuf[z] = jnp.concatenate([raw, raised], axis=1).astype(BF16)

    pl.semaphore_wait(barrier, len(greeted))

    def ring_copy(k, slot):
        return pltpu.make_async_remote_copy(
            src_ref=zbuf.at[slot],
            dst_ref=zbuf.at[slot],
            send_sem=z_send.at[k],
            recv_sem=z_recv.at[k],
            device_id=ring_peer(k),
            device_id_type=MESH,
        )

    for k in range(1, RING):
        ring_copy(k, z).start()

    def dens_copy(i):
        device, first, row = neighbours[i]
        return pltpu.make_async_remote_copy(
            src_ref=dens_win.at[mid, pl.ds(0, COLS), :],
            dst_ref=dens_win.at[pl.ds(first, LEAVES), pl.ds(row, COLS), :],
            send_sem=d_send.at[i],
            recv_sem=d_recv.at[i],
            device_id=device,
            device_id_type=MESH,
        )

    def lc_copy(i):
        device, first, row = neighbours[i]
        return pltpu.make_async_remote_copy(
            src_ref=lc_win.at[pl.ds(LEAVES // 2, LEAVES // 2), pl.ds(0, COLS), :],
            dst_ref=lc_win.at[pl.ds(first // 2, LEAVES // 2), pl.ds(row, COLS), :],
            send_sem=l_send.at[i],
            recv_sem=l_recv.at[i],
            device_id=device,
            device_id_type=MESH,
        )

    for i in range(5):
        lc_copy(i).start()
    for i in range(5):
        dens_copy(i).start()

    def one_hot(target, count):
        column = lax.broadcasted_iota(jnp.int32, (target.shape[0], count), 1)
        return (column == target).astype(F32).astype(BF16)

    row16 = lax.broadcasted_iota(jnp.int32, (16, 1), 0)
    target = jnp.where(
        row16 < 4,
        60 + 4 * group + row16,
        jnp.where(
            row16 < 6,
            24 + 2 * group + row16,
            jnp.where(row16 == 6, 12 + group, jnp.where(row16 == 7, 4 + group // 2, group // 4)),
        ),
    )
    pick_up = one_hot(target, upu_v.shape[2])
    half = RANK // 2

    def extract(pick, source, dest, rows):
        def step(r, carry):
            slab = jnp.concatenate([source[r], source[r + half]], axis=0)
            dest[pl.ds(pl.multiple_of(r * rows, rows), rows), :] = dot_nt(pick, slab)
            return carry

        lax.fori_loop(0, half, step, 0, unroll=8)

    load[4].wait()
    extract(pick_up, upu_v, sel_up, 16)

    def matrix_up(k):
        m = sel_up[pl.ds(k, half, stride=16), :]
        return jnp.concatenate([m[:, :RANK], m[:, RANK:]], axis=0)

    blank = jnp.zeros((RANK, RANK), F32)

    def placed(m, low_in, low_out):
        wide = jnp.concatenate([m, blank] if low_out else [blank, m], axis=1)
        none = jnp.zeros((RANK, 2 * RANK), F32)
        return jnp.concatenate([wide, none] if low_in else [none, wide], axis=0).astype(BF16)

    up = [placed(matrix_up(k), False, False) for k in range(7)]
    up.append(placed(matrix_up(7), False, True))
    up.append(placed(matrix_up(8), True, False))

    for k in range(1, RING):
        ring_copy(k, (z + RING - k) % RING).wait_recv()
    held = [zbuf[i].astype(F32) for i in range(RING)]
    c64 = [held[2 * i] + held[2 * i + 1] for i in range(4)]
    b64 = [c.astype(BF16) for c in c64]
    c32 = [
        dot(
            jnp.concatenate([b64[2 * a], b64[2 * a + 1]], axis=1),
            jnp.concatenate([up[2 * a], up[2 * a + 1]], axis=0),
        )
        for a in range(2)
    ]
    c16 = dot(
        jnp.concatenate([c.astype(BF16) for c in c32], axis=1),
        jnp.concatenate([up[4], up[5]], axis=0),
    )
    c8 = dot(c16.astype(BF16), up[6])
    c4 = dot(c8.astype(BF16), up[7])
    c2 = dot(c4.astype(BF16), up[8])
    low = lax.broadcasted_iota(jnp.int32, (COLS, 2 * RANK), 1) < RANK
    for i, c in enumerate(c64 + c32 + [c16, c8]):
        tab[group, i] = jnp.where(low, held[i], c).astype(BF16)
    tab[group, 8] = (c4 + c2).astype(BF16)

    def plane_copy(k, slot):
        return pltpu.make_async_remote_copy(
            src_ref=tab.at[slot],
            dst_ref=tab.at[slot],
            send_sem=p_send.at[k],
            recv_sem=p_recv.at[k],
            device_id=plane_peer(k),
            device_id_type=MESH,
        )

    for k in range(1, PLANE):
        plane_copy(k, group).start()

    for i in range(5):
        lc_copy(i).wait_recv()
    for i in range(5):
        dens_copy(i).wait_recv()
    load[6].wait()
    load[7].wait()
    base = leaf * LEAVES - LEAVES
    for i in range(LEAVES // 2):
        far = []
        for t in (2 * i, 2 * i + 1):
            near_sum = far_sum = None
            for j in range(3):
                column = within(near_idx[j, t] - base, 0, 3 * LEAVES - 1)
                near_term = dot_nt(dens_win[column], near_v[t, j])
                near_sum = near_term if near_sum is None else near_sum + near_term
                source = within(leaf_idx[j, t] - base, 0, 3 * LEAVES - 1)
                tile = lc_win[source // 2].astype(F32)
                turned = jnp.concatenate([tile[:, RANK:], tile[:, :RANK]], axis=1)
                chosen = jnp.where(source % 2 == 1, turned, tile)[:, :RANK].astype(BF16)
                far_term = dot_nt(chosen, lcoup_v[t, j])
                far_sum = far_term if far_sum is None else far_sum + far_term
            near_own[t] = near_sum[:COLS]
            near_out[t] = near_sum[COLS:].astype(BF16)
            far.append(far_sum)
        pair = jnp.concatenate(far, axis=1)
        far_own[i] = pair[:COLS]
        far_out[i] = pair[COLS:].astype(BF16)

    partner = {"leaf": leaf, "sub": other}
    swaps = [
        pltpu.make_async_remote_copy(
            src_ref=src,
            dst_ref=dst,
            send_sem=x_send.at[i],
            recv_sem=x_recv.at[i],
            device_id=partner,
            device_id_type=MESH,
        )
        for i, (src, dst) in enumerate(((near_out, near_in), (far_out, far_in)))
    ]
    for copy in swaps:
        copy.start()

    row8 = lax.broadcasted_iota(jnp.int32, (8, 1), 0)
    top = DEVS + leaf
    node_of = jnp.zeros((8, 1), jnp.int32)
    for k in range(6):
        node_of = jnp.where(row8 == k, top // (2 << k), node_of)
    load[5].wait()
    load[8].wait()
    pick_c = one_hot(node_of - 2, upc_v.shape[3])
    pick_d = one_hot(node_of - 4, upd_v.shape[2])
    for j in range(4):
        extract(pick_c, upc_v.at[j], sel_c.at[j], 8)
    extract(pick_d, upd_v, sel_d, 8)

    low64 = lax.broadcasted_iota(jnp.int32, (RANK, 2 * RANK), 1) < RANK

    def coupling(k, low_in):
        parts = []
        for j in range(4):
            m = sel_c[j, pl.ds(k, half, stride=8), :]
            turned = jnp.concatenate([m[:, RANK:], m[:, :RANK]], axis=1)
            both = jnp.concatenate([m, turned] if low_in else [turned, m], axis=0)
            parts.append(jnp.where(low64 == low_in, both, 0.0).astype(BF16))
        return jnp.concatenate(parts, axis=1)

    couplings = [coupling(k, k == 4) for k in range(6)]
    load[9].wait()
    load[10].wait()
    blank_b = jnp.zeros((RANK, RANK), BF16)
    near_coupling = jnp.concatenate(
        [m for j in range(4) for m in (ncoup_v[0, j], blank_b)], axis=1
    )
    chain = [ndown_v[0]]
    for k in range(5):
        m = sel_d[pl.ds(k, half, stride=8), :]
        down = jnp.concatenate([m[:, :RANK], m[:, RANK:]], axis=0).astype(BF16)
        chain.append(dot(chain[-1], down).astype(BF16))
    load[11].wait()
    load[12].wait()

    for k in range(1, PLANE):
        plane_copy(k, (group + PLANE - k) % PLANE).wait_recv()

    def source_tile(k, j):
        n = within(upper_idx[j, top // (2 << k) - 2], 64 >> k, (128 >> k) - 1)
        if k == 0:
            return tab[(n - 64) // 4, n % 4]
        if k == 1:
            return tab[(n - 32) // 2, 4 + n % 2]
        if k == 2:
            return tab[n - 16, 6]
        count = 1 << (k - 2)
        first = (n - (64 >> k)) * count
        total = None
        for i in range(count):
            part = tab[first + i, 7 if k == 3 else 8].astype(F32)
            total = part if total is None else total + part
        return total.astype(BF16)

    def node_tile(j):
        n = within(node_idx[0, j], 0, DEVS - 1)
        return tab[n // RING, n % RING]

    field = dot_nt(jnp.concatenate([node_tile(j) for j in range(4)], axis=1), near_coupling)
    for k in range(6):
        part = dot_nt(
            jnp.concatenate([source_tile(k, j) for j in range(4)], axis=1), couplings[k]
        )
        field = field + dot_nt(part.astype(BF16), chain[k])
    descended = dot_nt(field.astype(BF16), ldown_v[...].reshape(LEAVES * RANK, RANK))

    for copy in swaps:
        copy.wait_recv()
    for i in range(LEAVES // 2):
        pair = descended[:, 2 * RANK * i : 2 * RANK * (i + 1)]
        pair = pair + far_own[i] + far_in[i].astype(F32)
        stacked = jnp.concatenate(
            [jnp.where(low, pair, 0.0), jnp.where(low, 0.0, pair)], axis=0
        ).astype(BF16)
        farther = dot(stacked, rowb_v[2 * i : 2 * i + 2].reshape(2 * RANK, rowb_v.shape[2]))
        for h in range(2):
            t = 2 * i + h
            total = farther[h * COLS : (h + 1) * COLS] + near_own[t] + near_in[t].astype(F32)
            out_ref[t] = total.astype(BF16)

    for k in range(1, RING):
        ring_copy(k, z).wait_send()
    for k in range(1, PLANE):
        plane_copy(k, group).wait_send()
    for i in range(5):
        dens_copy(i).wait_send()
        lc_copy(i).wait_send()
    for copy in swaps:
        copy.wait_send()


def body(
    density,
    near_blocks,
    near_index,
    col_basis,
    row_basis,
    leaf_coupling,
    leaf_list,
    leaf_up,
    leaf_down,
    node_coupling,
    node_list,
    node_up,
    node_down,
    upper_coupling,
    upper_list,
    upper_up,
    upper_down,
):
    args = (
        jnp.swapaxes(density, 1, 2),
        near_blocks,
        near_index.T,
        jnp.swapaxes(col_basis, 1, 2),
        jnp.swapaxes(row_basis, 1, 2),
        leaf_coupling,
        leaf_list.T,
        leaf_up,
        leaf_down,
        node_coupling,
        node_list,
        node_up,
        node_down,
        jnp.transpose(upper_coupling, (1, 2, 3, 0)),
        upper_list.T,
        jnp.transpose(upper_up, (1, 2, 0)),
        jnp.transpose(upper_down, (1, 2, 0)),
    )
    held = pl.BlockSpec(memory_space=pltpu.HBM)
    small = pl.BlockSpec(memory_space=pltpu.SMEM)
    specs = [small if a.dtype == jnp.int32 else held for a in args]
    points = density.shape[1]
    dma = pltpu.SemaphoreType.DMA

    def like(i):
        return pltpu.VMEM(args[i].shape, args[i].dtype)

    result = pl.pallas_call(
        kernel,
        out_shape=jax.ShapeDtypeStruct((LEAVES, COLS, points), BF16),
        in_specs=specs,
        out_specs=pl.BlockSpec(memory_space=pltpu.VMEM),
        scratch_shapes=[
            pltpu.VMEM((3 * LEAVES, 2 * COLS, points), BF16),
            like(1),
            like(3),
            like(4),
            like(5),
            like(7),
            like(8),
            like(9),
            like(11),
            like(12),
            like(13),
            like(15),
            like(16),
            pltpu.VMEM((3 * LEAVES // 2, 2 * COLS, 2 * RANK), BF16),
            pltpu.VMEM((RING, COLS, 2 * RANK), BF16),
            pltpu.VMEM((PLANE, TILES, COLS, 2 * RANK), BF16),
            pltpu.VMEM((16 * RANK // 2, 2 * RANK), F32),
            pltpu.VMEM((4, 8 * RANK // 2, 2 * RANK), F32),
            pltpu.VMEM((8 * RANK // 2, 2 * RANK), F32),
            pltpu.VMEM((LEAVES, COLS, points), F32),
            pltpu.VMEM((LEAVES, COLS, points), BF16),
            pltpu.VMEM((LEAVES, COLS, points), BF16),
            pltpu.VMEM((LEAVES // 2, COLS, 2 * RANK), F32),
            pltpu.VMEM((LEAVES // 2, COLS, 2 * RANK), BF16),
            pltpu.VMEM((LEAVES // 2, COLS, 2 * RANK), BF16),
            dma((13,)),
            dma((RING,)),
            dma((RING,)),
            dma((PLANE,)),
            dma((PLANE,)),
            dma((5,)),
            dma((5,)),
            dma((5,)),
            dma((5,)),
            dma((2,)),
            dma((2,)),
        ],
        compiler_params=pltpu.CompilerParams(
            collective_id=0, has_side_effects=True, vmem_limit_bytes=60 << 20
        ),
        name="product",
    )(*args)
    return jnp.swapaxes(result, 1, 2)


def solution(mesh):
    placed = (
        P("leaf", None, "sub"),
        P("leaf", "sub", None, None),
        P("leaf", "sub"),
        P("leaf", None, None),
        P("leaf", None, None),
        P("leaf", "sub", None, None),
        P("leaf", "sub"),
        P("leaf", None, None),
        P("leaf", None, None),
        P("leaf", None, None, None),
        P("leaf", None),
        P("leaf", None, None),
        P("leaf", None, None),
        P(),
        P(),
        P(),
        P(),
    )
    return jax.shard_map(
        body, mesh=mesh, in_specs=placed, out_specs=P("leaf", None, "sub"), check_vma=False
    )
```

time: 901 us -> 30.6 us (0.03)
  blocking collectives: 604 us -> 0 us
  waiting for transfers between devices: 124 us -> 0 us
  local copies, waits for them, and re-layouts: 103 us -> 1.47 us
  matrix products: 31.2 us -> 0 us
  Pallas kernels: 0 us -> 28.9 us
  between operations: 13.7 us -> 0.01 us
  starting transfers between devices: 11.9 us -> 0 us
  other arithmetic: 10.8 us -> 0 us
    all_gather x3 -> x0, blocking collectives: 604 us -> none  [the longest x1 305 us: body(): lax.all_gather(node_coeff[None], 'leaf', axis=0, tiled=True)]
    reduce_scatter x2 -> x0, waiting for transfers between devices: 124 us -> none  [the longest x1 108 us: body(): lax.psum_scatter(far_part.astype(jnp.bfloat16), 'sub', scatter_dimension=...]
    unnamed x56 -> x1, local copies, waits for them, and re-layouts: 59 us -> 1.47 us
    dot_general x24 -> x0, matrix products: 31.2 us -> none  [the longest x6 8.73 us: upper_tree(): jnp.einsum('nfrs,nfsc->nrc', upper_coupling[breadth - 2:2 * breadth - 2],...]
    slice x13 -> x0, local copies, waits for them, and re-layouts: 29.7 us -> none  [the longest x5 16 us: upper_tree(): upper_coupling[breadth - 2:2 * breadth - 2]]
    pallas_call x0 -> x1, Pallas kernels: none -> 28.9 us  [body(): pl.pallas_call(kernel, out_shape=jax.ShapeDtypeStruct((LEAVES, COLS, poin...]
    gather x9 -> x0, local copies, waits for them, and re-layouts: 12.3 us -> none  [the longest x6 8.62 us: upper_tree(): sources = coeffs[height][listed]]
    ppermute x4 -> x0, starting transfers between devices: 11.8 us -> none  [the longest x2 9.25 us: extended_2(): lax.ppermute(lax.slice_in_dim(block, block.shape[dim] - width, None, axis...]
  transfers between devices with their start and end apart: 6 -> 0, of which waited for: 2 -> 0; matrix products, arithmetic and copies ran while one was open for 16% -> 0% of each run, Pallas kernels for 0% -> 0%
where the time goes in v1:
time: 30.6 us; the launch traced here: 30.4 us
  Pallas kernels  28.9 us (94%)
  local copies, waits for them, and re-layouts  1.47 us (5%)
    pallas_call x1, Pallas kernels, body(): pl.pallas_call(kernel, out_shape=jax.ShapeDtypeStruct((LEAVES, COLS, poin...  28.9 us
    unnamed x1, local copies, waits for them, and re-layouts  1.47 us

profile of v1, /device:TPU:1, one launch (start us, length us, event | category | flops | bytes accessed | tf_op | source)
XLA Modules:
  0.0 30.4 jit_solution(8682104449982964972)
XLA Ops:
  0.0 28.9 %product.1 = bf16[8,16,256]{2,1,0:T(8,128)(2,1)} custom-call(bf16[8,16,256]{2,1,0:T(8,128)(2,1)} %bitcast.16, bf16[8,3,256,256]{3,2,1,0:T(8,128)(2,1)} %near_hbm.1, s32[3,8]{1,0:T(4,128)} %bitcast.17, bf16[8,64,256]{2,1,0:T(8,128)(2,1)} %bitcast.14, bf16[8,64,256]{2,1,0:T(8,128)(2,1)} %bitcast.15, bf16[8,3,64,64]{3,2,1,0:T(8,128)(2,1)} %lcoup_hbm.1, ...), custom_call_target="tpu_custom_call" | custom-call | tf_op jit(solution)/shard_map/product/pallas_call | solution.py:464
  29.0 1.5 %copy.19 = bf16[8,256,16]{1,2,0:T(8,128)(2,1)} copy(bf16[8,256,16]{1,2,0:T(8,128)(2,1)} %bitcast.13) | data formatting | bytes 131072

commit v2 on v1

--- a/solution.py
+++ b/solution.py
@@ -16,6 +16,8 @@
 PLANE = 16
 DEVS = RING * PLANE
 TILES = 9
+RING_ORDER = (4, 3, 5, 2, 6, 1, 7)
+PLANE_ORDER = (10, 6, 14, 9, 11, 2, 8, 5, 7, 13, 15, 1, 3, 4, 12)
 
 
 def dot(a, b):
@@ -111,7 +113,7 @@
     load = [
         pltpu.make_async_copy(src, dst, load_sem.at[i]) for i, (src, dst) in enumerate(loads)
     ]
-    for copy in load:
+    for copy in load[:5]:
         copy.start()
 
     def ring_peer(k):
@@ -121,19 +123,20 @@
         return {"leaf": ((group + k) % PLANE) * RING + z, "sub": sub}
 
     after, before = (leaf + 1) % DEVS, (leaf + DEVS - 1) % DEVS
-    neighbours = [
-        ({"leaf": leaf, "sub": other}, LEAVES, COLS),
-        ({"leaf": after, "sub": sub}, 0, 0),
-        ({"leaf": after, "sub": other}, 0, COLS),
-        ({"leaf": before, "sub": sub}, 2 * LEAVES, 0),
-        ({"leaf": before, "sub": other}, 2 * LEAVES, COLS),
+    partner = {"leaf": leaf, "sub": other}
+    moves = [
+        ({"leaf": after, "sub": sub}, LEAVES, 0, 0),
+        ({"leaf": before, "sub": sub}, LEAVES, 2 * LEAVES, 0),
+        (partner, LEAVES, LEAVES, COLS),
+        (partner, 0, 0, COLS),
+        (partner, 2 * LEAVES, 2 * LEAVES, COLS),
     ]
 
     barrier = pltpu.get_barrier_semaphore()
     greeted = (
-        [ring_peer(k) for k in range(1, RING)]
-        + [plane_peer(k) for k in range(1, PLANE)]
-        + [device for device, _, _ in neighbours]
+        [ring_peer(k) for k in RING_ORDER]
+        + [plane_peer(k) for k in PLANE_ORDER]
+        + [device for device, _, _, _ in moves[:3]]
     )
     for device in greeted:
         pl.semaphore_signal(barrier, inc=1, device_id=device, device_id_type=MESH)
@@ -150,6 +153,8 @@
         pairs.append(pair)
     load[2].wait()
     load[3].wait()
+    for copy in load[5:]:
+        copy.start()
     raw = dot(jnp.concatenate(pairs, axis=1), lup_v[...].reshape(LEAVES * RANK, RANK))
     raised = dot(raw.astype(BF16), nup_v[0])
     zbuf[z] = jnp.concatenate([raw, raised], axis=1).astype(BF16)
@@ -166,14 +171,14 @@
             device_id_type=MESH,
         )
 
-    for k in range(1, RING):
+    for k in RING_ORDER:
         ring_copy(k, z).start()
 
     def dens_copy(i):
-        device, first, row = neighbours[i]
+        device, here, there, row = moves[i]
         return pltpu.make_async_remote_copy(
-            src_ref=dens_win.at[mid, pl.ds(0, COLS), :],
-            dst_ref=dens_win.at[pl.ds(first, LEAVES), pl.ds(row, COLS), :],
+            src_ref=dens_win.at[pl.ds(here, LEAVES), pl.ds(0, COLS), :],
+            dst_ref=dens_win.at[pl.ds(there, LEAVES), pl.ds(row, COLS), :],
             send_sem=d_send.at[i],
             recv_sem=d_recv.at[i],
             device_id=device,
@@ -181,19 +186,18 @@
         )
 
     def lc_copy(i):
-        device, first, row = neighbours[i]
+        device, here, there, row = moves[i]
         return pltpu.make_async_remote_copy(
-            src_ref=lc_win.at[pl.ds(LEAVES // 2, LEAVES // 2), pl.ds(0, COLS), :],
-            dst_ref=lc_win.at[pl.ds(first // 2, LEAVES // 2), pl.ds(row, COLS), :],
+            src_ref=lc_win.at[pl.ds(here // 2, LEAVES // 2), pl.ds(0, COLS), :],
+            dst_ref=lc_win.at[pl.ds(there // 2, LEAVES // 2), pl.ds(row, COLS), :],
             send_sem=l_send.at[i],
             recv_sem=l_recv.at[i],
             device_id=device,
             device_id_type=MESH,
         )
 
-    for i in range(5):
+    for i in range(3):
         lc_copy(i).start()
-    for i in range(5):
         dens_copy(i).start()
 
     def one_hot(target, count):
@@ -273,12 +277,55 @@
             device_id_type=MESH,
         )
 
-    for k in range(1, PLANE):
+    for k in PLANE_ORDER:
         plane_copy(k, group).start()
-
-    for i in range(5):
+    for i in range(2):
         lc_copy(i).wait_recv()
-    for i in range(5):
+        lc_copy(3 + i).start()
+        dens_copy(i).wait_recv()
+        dens_copy(3 + i).start()
+
+    row8 = lax.broadcasted_iota(jnp.int32, (8, 1), 0)
+    top = DEVS + leaf
+    node_of = jnp.zeros((8, 1), jnp.int32)
+    for k in range(6):
+        node_of = jnp.where(row8 == k, top // (2 << k), node_of)
+    load[5].wait()
+    load[8].wait()
+    pick_c = one_hot(node_of - 2, upc_v.shape[3])
+    pick_d = one_hot(node_of - 4, upd_v.shape[2])
+    for j in range(4):
+        extract(pick_c, upc_v.at[j], sel_c.at[j], 8)
+    extract(pick_d, upd_v, sel_d, 8)
+
+    low64 = lax.broadcasted_iota(jnp.int32, (RANK, 2 * RANK), 1) < RANK
+
+    def coupling(k, low_in):
+        parts = []
+        for j in range(4):
+            m = sel_c[j, pl.ds(k, half, stride=8), :]
+            turned = jnp.concatenate([m[:, RANK:], m[:, :RANK]], axis=1)
+            both = jnp.concatenate([m, turned] if low_in else [turned, m], axis=0)
+            parts.append(jnp.where(low64 == low_in, both, 0.0).astype(BF16))
+        return jnp.concatenate(parts, axis=1)
+
+    couplings = [coupling(k, k == 4) for k in range(6)]
+    load[9].wait()
+    load[10].wait()
+    blank_b = jnp.zeros((RANK, RANK), BF16)
+    near_coupling = jnp.concatenate(
+        [m for j in range(4) for m in (ncoup_v[0, j], blank_b)], axis=1
+    )
+    chain = [ndown_v[0]]
+    for k in range(5):
+        m = sel_d[pl.ds(k, half, stride=8), :]
+        down = jnp.concatenate([m[:, :RANK], m[:, RANK:]], axis=0).astype(BF16)
+        chain.append(dot(chain[-1], down).astype(BF16))
+    load[11].wait()
+    load[12].wait()
+
+    for i in range(2, 5):
+        lc_copy(i).wait_recv()
         dens_copy(i).wait_recv()
     load[6].wait()
     load[7].wait()
@@ -304,7 +351,6 @@
         far_own[i] = pair[:COLS]
         far_out[i] = pair[COLS:].astype(BF16)
 
-    partner = {"leaf": leaf, "sub": other}
     swaps = [
         pltpu.make_async_remote_copy(
             src_ref=src,
@@ -318,45 +364,6 @@
     ]
     for copy in swaps:
         copy.start()
-
-    row8 = lax.broadcasted_iota(jnp.int32, (8, 1), 0)
-    top = DEVS + leaf
-    node_of = jnp.zeros((8, 1), jnp.int32)
-    for k in range(6):
-        node_of = jnp.where(row8 == k, top // (2 << k), node_of)
-    load[5].wait()
-    load[8].wait()
-    pick_c = one_hot(node_of - 2, upc_v.shape[3])
-    pick_d = one_hot(node_of - 4, upd_v.shape[2])
-    for j in range(4):
-        extract(pick_c, upc_v.at[j], sel_c.at[j], 8)
-    extract(pick_d, upd_v, sel_d, 8)
-
-    low64 = lax.broadcasted_iota(jnp.int32, (RANK, 2 * RANK), 1) < RANK
-
-    def coupling(k, low_in):
-        parts = []
-        for j in range(4):
-            m = sel_c[j, pl.ds(k, half, stride=8), :]
-            turned = jnp.concatenate([m[:, RANK:], m[:, :RANK]], axis=1)
-            both = jnp.concatenate([m, turned] if low_in else [turned, m], axis=0)
-            parts.append(jnp.where(low64 == low_in, both, 0.0).astype(BF16))
-        return jnp.concatenate(parts, axis=1)
-
-    couplings = [coupling(k, k == 4) for k in range(6)]
-    load[9].wait()
-    load[10].wait()
-    blank_b = jnp.zeros((RANK, RANK), BF16)
-    near_coupling = jnp.concatenate(
-        [m for j in range(4) for m in (ncoup_v[0, j], blank_b)], axis=1
-    )
-    chain = [ndown_v[0]]
-    for k in range(5):
-        m = sel_d[pl.ds(k, half, stride=8), :]
-        down = jnp.concatenate([m[:, :RANK], m[:, RANK:]], axis=0).astype(BF16)
-        chain.append(dot(chain[-1], down).astype(BF16))
-    load[11].wait()
-    load[12].wait()
 
     for k in range(1, PLANE):
         plane_copy(k, (group + PLANE - k) % PLANE).wait_recv()
@@ -463,7 +470,7 @@
 
     result = pl.pallas_call(
         kernel,
-        out_shape=jax.ShapeDtypeStruct((LEAVES, COLS, points), BF16),
+        out_shape=pltpu.VMEM((LEAVES, COLS, points), BF16),
         in_specs=specs,
         out_specs=pl.BlockSpec(memory_space=pltpu.VMEM),
         scratch_shapes=[

time: 30.6 us -> 27.5 us (0.90)
  Pallas kernels: 28.9 us -> 26.7 us
  local copies, waits for them, and re-layouts: 1.47 us -> 0.63 us
    pallas_call x1, Pallas kernels: 28.9 us -> 26.7 us  [body(): pl.pallas_call(kernel, out_shape=pltpu.VMEM((LEAVES, COLS, points), BF16)...]
    unnamed x1, local copies, waits for them, and re-layouts: 1.47 us -> 0.63 us
where the time goes in v2:
time: 27.5 us; the launch traced here: 27.4 us
  Pallas kernels  26.7 us (97%)
  local copies, waits for them, and re-layouts  0.63 us (2%)
    pallas_call x1, Pallas kernels, body(): pl.pallas_call(kernel, out_shape=pltpu.VMEM((LEAVES, COLS, points), BF16)...  26.7 us
    unnamed x1, local copies, waits for them, and re-layouts  0.63 us

profile of v2, /device:TPU:1, one launch (start us, length us, event | category | flops | bytes accessed | tf_op | source)
XLA Modules:
  0.0 27.4 jit_solution(3954637724058670936)
XLA Ops:
  0.0 26.7 %product.1 = bf16[8,16,256]{2,1,0:T(8,128)(2,1)S(1)} custom-call(bf16[8,16,256]{2,1,0:T(8,128)(2,1)} %bitcast.16, bf16[8,3,256,256]{3,2,1,0:T(8,128)(2,1)} %near_hbm.1, s32[3,8]{1,0:T(4,128)} %bitcast.17, bf16[8,64,256]{2,1,0:T(8,128)(2,1)} %bitcast.14, bf16[8,64,256]{2,1,0:T(8,128)(2,1)} %bitcast.15, bf16[8,3,64,64]{3,2,1,0:T(8,128)(2,1)} %lcoup_hbm.1, ...), custom_call_target="tpu_custom_call" | custom-call | tf_op jit(solution)/shard_map/product/pallas_call | solution.py:471
  26.7 0.6 %copy.19 = bf16[8,256,16]{1,2,0:T(8,128)(2,1)} copy(bf16[8,256,16]{1,2,0:T(8,128)(2,1)S(1)} %bitcast.10) | data formatting | bytes 131072

commit v3 on v2

--- a/solution.py
+++ b/solution.py
@@ -15,7 +15,7 @@
 RING = 8
 PLANE = 16
 DEVS = RING * PLANE
-TILES = 9
+TILES = 5
 RING_ORDER = (4, 3, 5, 2, 6, 1, 7)
 PLANE_ORDER = (10, 6, 14, 9, 11, 2, 8, 5, 7, 13, 15, 1, 3, 4, 12)
 
@@ -66,6 +66,8 @@
     upd_v,
     lc_win,
     zbuf,
+    pbuf,
+    rawtab,
     tab,
     sel_up,
     sel_c,
@@ -79,8 +81,12 @@
     load_sem,
     z_send,
     z_recv,
+    r_send,
+    r_recv,
     p_send,
     p_recv,
+    q_send,
+    q_recv,
     d_send,
     d_recv,
     l_send,
@@ -101,7 +107,7 @@
         (lup_hbm, lup_v),
         (nup_hbm, nup_v),
         (upu_hbm, upu_v),
-        (upc_hbm, upc_v),
+        (upc_hbm.at[pl.ds(2 * sub, 2)], upc_v),
         (near_hbm, near_v),
         (lcoup_hbm, lcoup_v),
         (upd_hbm, upd_v),
@@ -157,48 +163,9 @@
         copy.start()
     raw = dot(jnp.concatenate(pairs, axis=1), lup_v[...].reshape(LEAVES * RANK, RANK))
     raised = dot(raw.astype(BF16), nup_v[0])
-    zbuf[z] = jnp.concatenate([raw, raised], axis=1).astype(BF16)
-
-    pl.semaphore_wait(barrier, len(greeted))
-
-    def ring_copy(k, slot):
-        return pltpu.make_async_remote_copy(
-            src_ref=zbuf.at[slot],
-            dst_ref=zbuf.at[slot],
-            send_sem=z_send.at[k],
-            recv_sem=z_recv.at[k],
-            device_id=ring_peer(k),
-            device_id_type=MESH,
-        )
-
-    for k in RING_ORDER:
-        ring_copy(k, z).start()
-
-    def dens_copy(i):
-        device, here, there, row = moves[i]
-        return pltpu.make_async_remote_copy(
-            src_ref=dens_win.at[pl.ds(here, LEAVES), pl.ds(0, COLS), :],
-            dst_ref=dens_win.at[pl.ds(there, LEAVES), pl.ds(row, COLS), :],
-            send_sem=d_send.at[i],
-            recv_sem=d_recv.at[i],
-            device_id=device,
-            device_id_type=MESH,
-        )
-
-    def lc_copy(i):
-        device, here, there, row = moves[i]
-        return pltpu.make_async_remote_copy(
-            src_ref=lc_win.at[pl.ds(here // 2, LEAVES // 2), pl.ds(0, COLS), :],
-            dst_ref=lc_win.at[pl.ds(there // 2, LEAVES // 2), pl.ds(row, COLS), :],
-            send_sem=l_send.at[i],
-            recv_sem=l_recv.at[i],
-            device_id=device,
-            device_id_type=MESH,
-        )
-
-    for i in range(3):
-        lc_copy(i).start()
-        dens_copy(i).start()
+    tile = jnp.concatenate([raw, raised], axis=1).astype(BF16)
+    zbuf[z] = tile
+    pbuf[group] = tile
 
     def one_hot(target, count):
         column = lax.broadcasted_iota(jnp.int32, (target.shape[0], count), 1)
@@ -233,57 +200,70 @@
         return jnp.concatenate([m[:, :RANK], m[:, RANK:]], axis=0)
 
     blank = jnp.zeros((RANK, RANK), F32)
-
-    def placed(m, low_in, low_out):
-        wide = jnp.concatenate([m, blank] if low_out else [blank, m], axis=1)
-        none = jnp.zeros((RANK, 2 * RANK), F32)
-        return jnp.concatenate([wide, none] if low_in else [none, wide], axis=0).astype(BF16)
-
-    up = [placed(matrix_up(k), False, False) for k in range(7)]
-    up.append(placed(matrix_up(7), False, True))
-    up.append(placed(matrix_up(8), True, False))
-
-    for k in range(1, RING):
-        ring_copy(k, (z + RING - k) % RING).wait_recv()
-    held = [zbuf[i].astype(F32) for i in range(RING)]
-    c64 = [held[2 * i] + held[2 * i + 1] for i in range(4)]
-    b64 = [c.astype(BF16) for c in c64]
-    c32 = [
-        dot(
-            jnp.concatenate([b64[2 * a], b64[2 * a + 1]], axis=1),
-            jnp.concatenate([up[2 * a], up[2 * a + 1]], axis=0),
-        )
-        for a in range(2)
-    ]
-    c16 = dot(
-        jnp.concatenate([c.astype(BF16) for c in c32], axis=1),
-        jnp.concatenate([up[4], up[5]], axis=0),
-    )
-    c8 = dot(c16.astype(BF16), up[6])
-    c4 = dot(c8.astype(BF16), up[7])
-    c2 = dot(c4.astype(BF16), up[8])
-    low = lax.broadcasted_iota(jnp.int32, (COLS, 2 * RANK), 1) < RANK
-    for i, c in enumerate(c64 + c32 + [c16, c8]):
-        tab[group, i] = jnp.where(low, held[i], c).astype(BF16)
-    tab[group, 8] = (c4 + c2).astype(BF16)
-
-    def plane_copy(k, slot):
+    up = []
+    for k in range(4):
+        wide = [matrix_up(k), blank] if k < 2 else [blank, matrix_up(k)]
+        up += [jnp.zeros((RANK, 2 * RANK), F32), jnp.concatenate(wide, axis=1)]
+    first = jnp.concatenate(up, axis=0).astype(BF16)
+    second = [jnp.concatenate([matrix_up(4), matrix_up(5)], axis=0)]
+    for k in (6, 7, 8):
+        second.append(dot(second[-1].astype(BF16), matrix_up(k).astype(BF16)))
+    second = jnp.concatenate(second, axis=1).astype(BF16)
+    up = jnp.concatenate([first, dot(first, second).astype(BF16)], axis=1)
+
+    pl.semaphore_wait(barrier, len(greeted))
+
+    def ring_copy(k, slot):
         return pltpu.make_async_remote_copy(
-            src_ref=tab.at[slot],
-            dst_ref=tab.at[slot],
-            send_sem=p_send.at[k],
-            recv_sem=p_recv.at[k],
+            src_ref=zbuf.at[slot],
+            dst_ref=zbuf.at[slot],
+            send_sem=z_send.at[k],
+            recv_sem=z_recv.at[k],
+            device_id=ring_peer(k),
+            device_id_type=MESH,
+        )
+
+    for k in RING_ORDER:
+        ring_copy(k, z).start()
+
+    def raw_copy(k, slot):
+        return pltpu.make_async_remote_copy(
+            src_ref=pbuf.at[slot],
+            dst_ref=pbuf.at[slot],
+            send_sem=r_send.at[k],
+            recv_sem=r_recv.at[k],
             device_id=plane_peer(k),
             device_id_type=MESH,
         )
 
     for k in PLANE_ORDER:
-        plane_copy(k, group).start()
-    for i in range(2):
-        lc_copy(i).wait_recv()
-        lc_copy(3 + i).start()
-        dens_copy(i).wait_recv()
-        dens_copy(3 + i).start()
+        raw_copy(k, group).start()
+
+    def dens_copy(i):
+        device, here, there, row = moves[i]
+        return pltpu.make_async_remote_copy(
+            src_ref=dens_win.at[pl.ds(here, LEAVES), pl.ds(0, COLS), :],
+            dst_ref=dens_win.at[pl.ds(there, LEAVES), pl.ds(row, COLS), :],
+            send_sem=d_send.at[i],
+            recv_sem=d_recv.at[i],
+            device_id=device,
+            device_id_type=MESH,
+        )
+
+    def lc_copy(i):
+        device, here, there, row = moves[i]
+        return pltpu.make_async_remote_copy(
+            src_ref=lc_win.at[pl.ds(here // 2, LEAVES // 2), pl.ds(0, COLS), :],
+            dst_ref=lc_win.at[pl.ds(there // 2, LEAVES // 2), pl.ds(row, COLS), :],
+            send_sem=l_send.at[i],
+            recv_sem=l_recv.at[i],
+            device_id=device,
+            device_id_type=MESH,
+        )
+
+    for i in range(3):
+        lc_copy(i).start()
+        dens_copy(i).start()
 
     row8 = lax.broadcasted_iota(jnp.int32, (8, 1), 0)
     top = DEVS + leaf
@@ -294,28 +274,20 @@
     load[8].wait()
     pick_c = one_hot(node_of - 2, upc_v.shape[3])
     pick_d = one_hot(node_of - 4, upd_v.shape[2])
-    for j in range(4):
-        extract(pick_c, upc_v.at[j], sel_c.at[j], 8)
+    for j in range(2):
+        extract(pick_c, upc_v.at[j], sel_c.at[2 * sub + j], 8)
+    share = pltpu.make_async_remote_copy(
+        src_ref=sel_c.at[pl.ds(2 * sub, 2)],
+        dst_ref=sel_c.at[pl.ds(2 * sub, 2)],
+        send_sem=x_send.at[2],
+        recv_sem=x_recv.at[2],
+        device_id=partner,
+        device_id_type=MESH,
+    )
+    share.start()
     extract(pick_d, upd_v, sel_d, 8)
 
-    low64 = lax.broadcasted_iota(jnp.int32, (RANK, 2 * RANK), 1) < RANK
-
-    def coupling(k, low_in):
-        parts = []
-        for j in range(4):
-            m = sel_c[j, pl.ds(k, half, stride=8), :]
-            turned = jnp.concatenate([m[:, RANK:], m[:, :RANK]], axis=1)
-            both = jnp.concatenate([m, turned] if low_in else [turned, m], axis=0)
-            parts.append(jnp.where(low64 == low_in, both, 0.0).astype(BF16))
-        return jnp.concatenate(parts, axis=1)
-
-    couplings = [coupling(k, k == 4) for k in range(6)]
     load[9].wait()
-    load[10].wait()
-    blank_b = jnp.zeros((RANK, RANK), BF16)
-    near_coupling = jnp.concatenate(
-        [m for j in range(4) for m in (ncoup_v[0, j], blank_b)], axis=1
-    )
     chain = [ndown_v[0]]
     for k in range(5):
         m = sel_d[pl.ds(k, half, stride=8), :]
@@ -324,6 +296,80 @@
     load[11].wait()
     load[12].wait()
 
+    for k in range(1, PLANE):
+        raw_copy(k, (group + PLANE - k) % PLANE).wait_recv()
+    low = lax.broadcasted_iota(jnp.int32, (COLS, 2 * RANK), 1) < RANK
+
+    def turn(m):
+        return jnp.concatenate([m[:, RANK:], m[:, :RANK]], axis=1)
+
+    for i in range(PLANE // 2):
+        rawtab[z, i] = jnp.where(
+            low, pbuf[2 * i].astype(F32), turn(pbuf[2 * i + 1].astype(F32))
+        ).astype(BF16)
+
+    def along_copy(k, slot):
+        return pltpu.make_async_remote_copy(
+            src_ref=rawtab.at[slot],
+            dst_ref=rawtab.at[slot],
+            send_sem=q_send.at[k],
+            recv_sem=q_recv.at[k],
+            device_id=ring_peer(k),
+            device_id_type=MESH,
+        )
+
+    for k in RING_ORDER:
+        along_copy(k, z).start()
+
+    for k in range(1, RING):
+        ring_copy(k, (z + RING - k) % RING).wait_recv()
+    c64 = [zbuf[2 * i].astype(F32) + zbuf[2 * i + 1].astype(F32) for i in range(4)]
+    sums = dot(jnp.concatenate([c.astype(BF16) for c in c64], axis=1), up)
+    tab[group, 0] = jnp.where(low, turn(c64[0]), c64[1]).astype(BF16)
+    tab[group, 1] = jnp.where(low, turn(c64[2]), c64[3]).astype(BF16)
+    for i in range(3):
+        tab[group, 2 + i] = sums[:, 2 * RANK * i : 2 * RANK * (i + 1)].astype(BF16)
+
+    def plane_copy(k, slot):
+        return pltpu.make_async_remote_copy(
+            src_ref=tab.at[slot],
+            dst_ref=tab.at[slot],
+            send_sem=p_send.at[k],
+            recv_sem=p_recv.at[k],
+            device_id=plane_peer(k),
+            device_id_type=MESH,
+        )
+
+    for k in PLANE_ORDER:
+        plane_copy(k, group).start()
+    for i in range(2):
+        lc_copy(i).wait_recv()
+        lc_copy(3 + i).start()
+        dens_copy(i).wait_recv()
+        dens_copy(3 + i).start()
+
+    low64 = lax.broadcasted_iota(jnp.int32, (half, 2 * RANK), 1) < RANK
+
+    def coupling(k):
+        parts = []
+        for j in range(4):
+            m = sel_c[j, pl.ds(k, half, stride=8), :]
+            turned = jnp.concatenate([m[:, RANK:], m[:, :RANK]], axis=1)
+            both = [jnp.where(low64, m, turned), jnp.where(low64, turned, m)]
+            parts.append(jnp.concatenate(both, axis=0).astype(BF16))
+        return jnp.concatenate(parts, axis=1)
+
+    pltpu.make_async_remote_copy(
+        src_ref=sel_c.at[pl.ds(2 * other, 2)],
+        dst_ref=sel_c.at[pl.ds(2 * other, 2)],
+        send_sem=x_send.at[2],
+        recv_sem=x_recv.at[2],
+        device_id=partner,
+        device_id_type=MESH,
+    ).wait_recv()
+    couplings = [coupling(k) for k in range(6)]
+    load[10].wait()
+    near_coupling = jnp.concatenate([ncoup_v[0, j // 2] for j in range(8)], axis=1)
     for i in range(2, 5):
         lc_copy(i).wait_recv()
         dens_copy(i).wait_recv()
@@ -370,30 +416,39 @@
 
     def source_tile(k, j):
         n = within(upper_idx[j, top // (2 << k) - 2], 64 >> k, (128 >> k) - 1)
-        if k == 0:
-            return tab[(n - 64) // 4, n % 4]
-        if k == 1:
-            return tab[(n - 32) // 2, 4 + n % 2]
-        if k == 2:
-            return tab[n - 16, 6]
+        if k < 3:
+            place = (n - 64) // 4, n % 4 // 2
+            if k == 1:
+                place = (n - 32) // 2, 2
+            if k == 2:
+                place = n - 16, 3
+            total = tab[place[0], place[1]].astype(F32)
+            return jnp.where(low == (n % 2 == 0 if k < 2 else True), total, 0.0).astype(BF16)
         count = 1 << (k - 2)
         first = (n - (64 >> k)) * count
         total = None
         for i in range(count):
-            part = tab[first + i, 7 if k == 3 else 8].astype(F32)
+            part = tab[first + i, 3 if k == 3 else 4].astype(F32)
             total = part if total is None else total + part
-        return total.astype(BF16)
+        return jnp.where(low == (k == 4), total, 0.0).astype(BF16)
 
     def node_tile(j):
         n = within(node_idx[0, j], 0, DEVS - 1)
-        return tab[n // RING, n % RING]
-
-    field = dot_nt(jnp.concatenate([node_tile(j) for j in range(4)], axis=1), near_coupling)
+        tile = rawtab[n % RING, n // (2 * RING)].astype(F32)
+        return jnp.where(low == (n // RING % 2 == 0), tile, 0.0).astype(BF16)
+
+    field = None
     for k in range(6):
         part = dot_nt(
             jnp.concatenate([source_tile(k, j) for j in range(4)], axis=1), couplings[k]
         )
-        field = field + dot_nt(part.astype(BF16), chain[k])
+        part = dot_nt(part.astype(BF16), chain[k])
+        field = part if field is None else field + part
+    for k in range(1, RING):
+        along_copy(k, (z + RING - k) % RING).wait_recv()
+    field = field + dot_nt(
+        jnp.concatenate([node_tile(j) for j in range(4)], axis=1), near_coupling
+    )
     descended = dot_nt(field.astype(BF16), ldown_v[...].reshape(LEAVES * RANK, RANK))
 
     for copy in swaps:
@@ -412,12 +467,14 @@
 
     for k in range(1, RING):
         ring_copy(k, z).wait_send()
+        along_copy(k, z).wait_send()
     for k in range(1, PLANE):
+        raw_copy(k, group).wait_send()
         plane_copy(k, group).wait_send()
     for i in range(5):
         dens_copy(i).wait_send()
         lc_copy(i).wait_send()
-    for copy in swaps:
+    for copy in swaps + [share]:
         copy.wait_send()
 
 
@@ -484,11 +541,13 @@
             like(9),
             like(11),
             like(12),
-            like(13),
+            pltpu.VMEM((2,) + args[13].shape[1:], BF16),
             like(15),
             like(16),
             pltpu.VMEM((3 * LEAVES // 2, 2 * COLS, 2 * RANK), BF16),
             pltpu.VMEM((RING, COLS, 2 * RANK), BF16),
+            pltpu.VMEM((PLANE, COLS, 2 * RANK), BF16),
+            pltpu.VMEM((RING, PLANE // 2, COLS, 2 * RANK), BF16),
             pltpu.VMEM((PLANE, TILES, COLS, 2 * RANK), BF16),
             pltpu.VMEM((16 * RANK // 2, 2 * RANK), F32),
             pltpu.VMEM((4, 8 * RANK // 2, 2 * RANK), F32),
@@ -504,12 +563,16 @@
             dma((RING,)),
             dma((PLANE,)),
             dma((PLANE,)),
+            dma((PLANE,)),
+            dma((PLANE,)),
+            dma((RING,)),
+            dma((RING,)),
             dma((5,)),
             dma((5,)),
             dma((5,)),
             dma((5,)),
-            dma((2,)),
-            dma((2,)),
+            dma((3,)),
+            dma((3,)),
         ],
         compiler_params=pltpu.CompilerParams(
             collective_id=0, has_side_effects=True, vmem_limit_bytes=60 << 20

time: 27.5 us -> 25.2 us (0.916)
  Pallas kernels: 26.7 us -> 24.4 us
    pallas_call x1, Pallas kernels: 26.7 us -> 24.4 us  [body(): pl.pallas_call(kernel, out_shape=pltpu.VMEM((LEAVES, COLS, points), BF16)...]
where the time goes in v3:
time: 25.2 us; the launch traced here: 25.1 us
  Pallas kernels  24.4 us (97%)
  local copies, waits for them, and re-layouts  0.63 us (2%)
    pallas_call x1, Pallas kernels, body(): pl.pallas_call(kernel, out_shape=pltpu.VMEM((LEAVES, COLS, points), BF16)...  24.4 us
    unnamed x1, local copies, waits for them, and re-layouts  0.63 us

profile of v3, /device:TPU:1, one launch (start us, length us, event | category | flops | bytes accessed | tf_op | source)
XLA Modules:
  0.0 25.1 jit_solution(9047121649527648876)
XLA Ops:
  0.0 24.4 %product.1 = bf16[8,16,256]{2,1,0:T(8,128)(2,1)S(1)} custom-call(bf16[8,16,256]{2,1,0:T(8,128)(2,1)} %bitcast.16, bf16[8,3,256,256]{3,2,1,0:T(8,128)(2,1)} %near_hbm.1, s32[3,8]{1,0:T(4,128)} %bitcast.17, bf16[8,64,256]{2,1,0:T(8,128)(2,1)} %bitcast.14, bf16[8,64,256]{2,1,0:T(8,128)(2,1)} %bitcast.15, bf16[8,3,64,64]{3,2,1,0:T(8,128)(2,1)} %lcoup_hbm.1, ...), custom_call_target="tpu_custom_call" | custom-call | tf_op jit(solution)/shard_map/product/pallas_call | solution.py:528
  24.5 0.6 %copy.19 = bf16[8,256,16]{1,2,0:T(8,128)(2,1)} copy(bf16[8,256,16]{1,2,0:T(8,128)(2,1)S(1)} %bitcast.10) | data formatting | bytes 131072

commit v4 on v3

--- a/solution.py
+++ b/solution.py
@@ -107,7 +107,7 @@
         (lup_hbm, lup_v),
         (nup_hbm, nup_v),
         (upu_hbm, upu_v),
-        (upc_hbm.at[pl.ds(2 * sub, 2)], upc_v),
+        (upc_hbm, upc_v),
         (near_hbm, near_v),
         (lcoup_hbm, lcoup_v),
         (upd_hbm, upd_v),
@@ -185,12 +185,12 @@
     half = RANK // 2
 
     def extract(pick, source, dest, rows):
-        def step(r, carry):
-            slab = jnp.concatenate([source[r], source[r + half]], axis=0)
-            dest[pl.ds(pl.multiple_of(r * rows, rows), rows), :] = dot_nt(pick, slab)
-            return carry
-
-        lax.fori_loop(0, half, step, 0, unroll=8)
+        for r in range(0, half, 2):
+            slabs = [source[i] for i in (r, r + half, r + 1, r + 1 + half)]
+            both = dot_nt(pick, jnp.concatenate(slabs, axis=0))
+            for a in range(2):
+                first = (r + a) * rows
+                dest[first : first + rows, :] = both[:, 2 * RANK * a : 2 * RANK * (a + 1)]
 
     load[4].wait()
     extract(pick_up, upu_v, sel_up, 16)
@@ -236,9 +236,6 @@
             device_id_type=MESH,
         )
 
-    for k in PLANE_ORDER:
-        raw_copy(k, group).start()
-
     def dens_copy(i):
         device, here, there, row = moves[i]
         return pltpu.make_async_remote_copy(
@@ -264,6 +261,8 @@
     for i in range(3):
         lc_copy(i).start()
         dens_copy(i).start()
+    for k in PLANE_ORDER:
+        raw_copy(k, group).start()
 
     row8 = lax.broadcasted_iota(jnp.int32, (8, 1), 0)
     top = DEVS + leaf
@@ -274,17 +273,8 @@
     load[8].wait()
     pick_c = one_hot(node_of - 2, upc_v.shape[3])
     pick_d = one_hot(node_of - 4, upd_v.shape[2])
-    for j in range(2):
-        extract(pick_c, upc_v.at[j], sel_c.at[2 * sub + j], 8)
-    share = pltpu.make_async_remote_copy(
-        src_ref=sel_c.at[pl.ds(2 * sub, 2)],
-        dst_ref=sel_c.at[pl.ds(2 * sub, 2)],
-        send_sem=x_send.at[2],
-        recv_sem=x_recv.at[2],
-        device_id=partner,
-        device_id_type=MESH,
-    )
-    share.start()
+    for j in range(4):
+        extract(pick_c, upc_v.at[j], sel_c.at[j], 8)
     extract(pick_d, upd_v, sel_d, 8)
 
     load[9].wait()
@@ -296,30 +286,10 @@
     load[11].wait()
     load[12].wait()
 
-    for k in range(1, PLANE):
-        raw_copy(k, (group + PLANE - k) % PLANE).wait_recv()
     low = lax.broadcasted_iota(jnp.int32, (COLS, 2 * RANK), 1) < RANK
 
     def turn(m):
         return jnp.concatenate([m[:, RANK:], m[:, :RANK]], axis=1)
-
-    for i in range(PLANE // 2):
-        rawtab[z, i] = jnp.where(
-            low, pbuf[2 * i].astype(F32), turn(pbuf[2 * i + 1].astype(F32))
-        ).astype(BF16)
-
-    def along_copy(k, slot):
-        return pltpu.make_async_remote_copy(
-            src_ref=rawtab.at[slot],
-            dst_ref=rawtab.at[slot],
-            send_sem=q_send.at[k],
-            recv_sem=q_recv.at[k],
-            device_id=ring_peer(k),
-            device_id_type=MESH,
-        )
-
-    for k in RING_ORDER:
-        along_copy(k, z).start()
 
     for k in range(1, RING):
         ring_copy(k, (z + RING - k) % RING).wait_recv()
@@ -342,6 +312,26 @@
 
     for k in PLANE_ORDER:
         plane_copy(k, group).start()
+    for k in range(1, PLANE):
+        raw_copy(k, (group + PLANE - k) % PLANE).wait_recv()
+    for i in range(PLANE // 2):
+        rawtab[z, i] = jnp.where(
+            low, pbuf[2 * i].astype(F32), turn(pbuf[2 * i + 1].astype(F32))
+        ).astype(BF16)
+
+    def along_copy(k, slot):
+        return pltpu.make_async_remote_copy(
+            src_ref=rawtab.at[slot],
+            dst_ref=rawtab.at[slot],
+            send_sem=q_send.at[k],
+            recv_sem=q_recv.at[k],
+            device_id=ring_peer(k),
+            device_id_type=MESH,
+        )
+
+    for k in RING_ORDER:
+        along_copy(k, z).start()
+
     for i in range(2):
         lc_copy(i).wait_recv()
         lc_copy(3 + i).start()
@@ -359,14 +349,6 @@
             parts.append(jnp.concatenate(both, axis=0).astype(BF16))
         return jnp.concatenate(parts, axis=1)
 
-    pltpu.make_async_remote_copy(
-        src_ref=sel_c.at[pl.ds(2 * other, 2)],
-        dst_ref=sel_c.at[pl.ds(2 * other, 2)],
-        send_sem=x_send.at[2],
-        recv_sem=x_recv.at[2],
-        device_id=partner,
-        device_id_type=MESH,
-    ).wait_recv()
     couplings = [coupling(k) for k in range(6)]
     load[10].wait()
     near_coupling = jnp.concatenate([ncoup_v[0, j // 2] for j in range(8)], axis=1)
@@ -474,7 +456,7 @@
     for i in range(5):
         dens_copy(i).wait_send()
         lc_copy(i).wait_send()
-    for copy in swaps + [share]:
+    for copy in swaps:
         copy.wait_send()
 
 
@@ -541,7 +523,7 @@
             like(9),
             like(11),
             like(12),
-            pltpu.VMEM((2,) + args[13].shape[1:], BF16),
+            like(13),
             like(15),
             like(16),
             pltpu.VMEM((3 * LEAVES // 2, 2 * COLS, 2 * RANK), BF16),
@@ -571,8 +553,8 @@
             dma((5,)),
             dma((5,)),
             dma((5,)),
-            dma((3,)),
-            dma((3,)),
+            dma((2,)),
+            dma((2,)),
         ],
         compiler_params=pltpu.CompilerParams(
             collective_id=0, has_side_effects=True, vmem_limit_bytes=60 << 20

time: 25.2 us -> 24.4 us (0.968)
  Pallas kernels: 24.4 us -> 23.7 us
    pallas_call x1, Pallas kernels: 24.4 us -> 23.7 us  [body(): pl.pallas_call(kernel, out_shape=pltpu.VMEM((LEAVES, COLS, points), BF16)...]
where the time goes in v4:
time: 24.4 us; the launch traced here: 24.3 us
  Pallas kernels  23.7 us (97%)
  local copies, waits for them, and re-layouts  0.63 us (3%)
    pallas_call x1, Pallas kernels, body(): pl.pallas_call(kernel, out_shape=pltpu.VMEM((LEAVES, COLS, points), BF16)...  23.7 us
    unnamed x1, local copies, waits for them, and re-layouts  0.63 us

profile of v4, /device:TPU:1, one launch (start us, length us, event | category | flops | bytes accessed | tf_op | source)
XLA Modules:
  0.0 24.3 jit_solution(2527169617041690926)
XLA Ops:
  0.0 23.7 %product.1 = bf16[8,16,256]{2,1,0:T(8,128)(2,1)S(1)} custom-call(bf16[8,16,256]{2,1,0:T(8,128)(2,1)} %bitcast.16, bf16[8,3,256,256]{3,2,1,0:T(8,128)(2,1)} %near_hbm.1, s32[3,8]{1,0:T(4,128)} %bitcast.17, bf16[8,64,256]{2,1,0:T(8,128)(2,1)} %bitcast.14, bf16[8,64,256]{2,1,0:T(8,128)(2,1)} %bitcast.15, bf16[8,3,64,64]{3,2,1,0:T(8,128)(2,1)} %lcoup_hbm.1, ...), custom_call_target="tpu_custom_call" | custom-call | tf_op jit(solution)/shard_map/product/pallas_call | solution.py:510
  23.7 0.6 %copy.19 = bf16[8,256,16]{1,2,0:T(8,128)(2,1)} copy(bf16[8,256,16]{1,2,0:T(8,128)(2,1)S(1)} %bitcast.10) | data formatting | bytes 131072

commit v5 on v4

--- a/solution.py
+++ b/solution.py
@@ -35,22 +35,26 @@
 def kernel(
     dens_hbm,
     near_hbm,
-    near_idx,
+    near_idx_hbm,
     colb_hbm,
     rowb_hbm,
     lcoup_hbm,
-    leaf_idx,
+    leaf_idx_hbm,
     lup_hbm,
     ldown_hbm,
     ncoup_hbm,
-    node_idx,
+    node_idx_hbm,
     nup_hbm,
     ndown_hbm,
     upc_hbm,
-    upper_idx,
+    upper_idx_hbm,
     upu_hbm,
     upd_hbm,
     out_ref,
+    near_idx,
+    leaf_idx,
+    node_idx,
+    upper_idx,
     dens_win,
     near_v,
     colb_v,
@@ -69,6 +73,7 @@
     pbuf,
     rawtab,
     tab,
+    last_v,
     sel_up,
     sel_c,
     sel_d,
@@ -115,6 +120,10 @@
         (ncoup_hbm, ncoup_v),
         (ldown_hbm, ldown_v),
         (rowb_hbm, rowb_v),
+        (near_idx_hbm, near_idx),
+        (leaf_idx_hbm, leaf_idx),
+        (node_idx_hbm, node_idx),
+        (upper_idx_hbm, upper_idx),
     ]
     load = [
         pltpu.make_async_copy(src, dst, load_sem.at[i]) for i, (src, dst) in enumerate(loads)
@@ -283,8 +292,6 @@
         m = sel_d[pl.ds(k, half, stride=8), :]
         down = jnp.concatenate([m[:, :RANK], m[:, RANK:]], axis=0).astype(BF16)
         chain.append(dot(chain[-1], down).astype(BF16))
-    load[11].wait()
-    load[12].wait()
 
     low = lax.broadcasted_iota(jnp.int32, (COLS, 2 * RANK), 1) < RANK
 
@@ -352,11 +359,19 @@
     couplings = [coupling(k) for k in range(6)]
     load[10].wait()
     near_coupling = jnp.concatenate([ncoup_v[0, j // 2] for j in range(8)], axis=1)
+    load[11].wait()
+    load[12].wait()
+    points = rowb_v.shape[2]
+    for t in range(LEAVES):
+        last_v[:, t * points : (t + 1) * points] = lax.dot_general(
+            ldown_v[t], rowb_v[t], (((0,), (0,)), ((), ())), preferred_element_type=F32
+        ).astype(BF16)
+
     for i in range(2, 5):
         lc_copy(i).wait_recv()
         dens_copy(i).wait_recv()
-    load[6].wait()
-    load[7].wait()
+    for i in (6, 7, 13, 14, 15, 16):
+        load[i].wait()
     base = leaf * LEAVES - LEAVES
     for i in range(LEAVES // 2):
         far = []
@@ -393,6 +408,18 @@
     for copy in swaps:
         copy.start()
 
+    for copy in swaps:
+        copy.wait_recv()
+    for i in range(LEAVES // 2):
+        pair = far_own[i] + far_in[i].astype(F32)
+        stacked = jnp.concatenate(
+            [jnp.where(low, pair, 0.0), jnp.where(low, 0.0, pair)], axis=0
+        ).astype(BF16)
+        farther = dot(stacked, rowb_v[2 * i : 2 * i + 2].reshape(2 * RANK, points))
+        for h in range(2):
+            t = 2 * i + h
+            near_own[t] += farther[h * COLS : (h + 1) * COLS] + near_in[t].astype(F32)
+
     for k in range(1, PLANE):
         plane_copy(k, (group + PLANE - k) % PLANE).wait_recv()
 
@@ -431,21 +458,9 @@
     field = field + dot_nt(
         jnp.concatenate([node_tile(j) for j in range(4)], axis=1), near_coupling
     )
-    descended = dot_nt(field.astype(BF16), ldown_v[...].reshape(LEAVES * RANK, RANK))
-
-    for copy in swaps:
-        copy.wait_recv()
-    for i in range(LEAVES // 2):
-        pair = descended[:, 2 * RANK * i : 2 * RANK * (i + 1)]
-        pair = pair + far_own[i] + far_in[i].astype(F32)
-        stacked = jnp.concatenate(
-            [jnp.where(low, pair, 0.0), jnp.where(low, 0.0, pair)], axis=0
-        ).astype(BF16)
-        farther = dot(stacked, rowb_v[2 * i : 2 * i + 2].reshape(2 * RANK, rowb_v.shape[2]))
-        for h in range(2):
-            t = 2 * i + h
-            total = farther[h * COLS : (h + 1) * COLS] + near_own[t] + near_in[t].astype(F32)
-            out_ref[t] = total.astype(BF16)
+    last = dot(field.astype(BF16), last_v[...])
+    for t in range(LEAVES):
+        out_ref[t] = (near_own[t] + last[:, t * points : (t + 1) * points]).astype(BF16)
 
     for k in range(1, RING):
         ring_copy(k, z).wait_send()
@@ -499,13 +514,15 @@
         jnp.transpose(upper_down, (1, 2, 0)),
     )
     held = pl.BlockSpec(memory_space=pltpu.HBM)
-    small = pl.BlockSpec(memory_space=pltpu.SMEM)
-    specs = [small if a.dtype == jnp.int32 else held for a in args]
+    specs = [held] * len(args)
     points = density.shape[1]
     dma = pltpu.SemaphoreType.DMA
 
     def like(i):
         return pltpu.VMEM(args[i].shape, args[i].dtype)
+
+    def small(i):
+        return pltpu.SMEM(args[i].shape, args[i].dtype)
 
     result = pl.pallas_call(
         kernel,
@@ -513,6 +530,10 @@
         in_specs=specs,
         out_specs=pl.BlockSpec(memory_space=pltpu.VMEM),
         scratch_shapes=[
+            small(2),
+            small(6),
+            small(10),
+            small(14),
             pltpu.VMEM((3 * LEAVES, 2 * COLS, points), BF16),
             like(1),
             like(3),
@@ -531,6 +552,7 @@
             pltpu.VMEM((PLANE, COLS, 2 * RANK), BF16),
             pltpu.VMEM((RING, PLANE // 2, COLS, 2 * RANK), BF16),
             pltpu.VMEM((PLANE, TILES, COLS, 2 * RANK), BF16),
+            pltpu.VMEM((RANK, LEAVES * points), BF16),
             pltpu.VMEM((16 * RANK // 2, 2 * RANK), F32),
             pltpu.VMEM((4, 8 * RANK // 2, 2 * RANK), F32),
             pltpu.VMEM((8 * RANK // 2, 2 * RANK), F32),
@@ -540,7 +562,7 @@
             pltpu.VMEM((LEAVES // 2, COLS, 2 * RANK), F32),
             pltpu.VMEM((LEAVES // 2, COLS, 2 * RANK), BF16),
             pltpu.VMEM((LEAVES // 2, COLS, 2 * RANK), BF16),
-            dma((13,)),
+            dma((17,)),
             dma((RING,)),
             dma((RING,)),
             dma((PLANE,)),

time: 24.4 us -> 23.7 us (0.971)
  Pallas kernels: 23.7 us -> 22.9 us
    pallas_call x1, Pallas kernels: 23.7 us -> 22.9 us  [body(): pl.pallas_call(kernel, out_shape=pltpu.VMEM((LEAVES, COLS, points), BF16)...]
where the time goes in v5:
time: 23.7 us; the launch traced here: 23.6 us
  Pallas kernels  22.9 us (97%)
  local copies, waits for them, and re-layouts  0.63 us (3%)
    pallas_call x1, Pallas kernels, body(): pl.pallas_call(kernel, out_shape=pltpu.VMEM((LEAVES, COLS, points), BF16)...  22.9 us
    unnamed x1, local copies, waits for them, and re-layouts  0.63 us

profile of v5, /device:TPU:1, one launch (start us, length us, event | category | flops | bytes accessed | tf_op | source)
XLA Modules:
  0.0 23.6 jit_solution(6589482837266944583)
XLA Ops:
  0.0 22.9 %product.1 = bf16[8,16,256]{2,1,0:T(8,128)(2,1)S(1)} custom-call(bf16[8,16,256]{2,1,0:T(8,128)(2,1)} %bitcast.16, bf16[8,3,256,256]{3,2,1,0:T(8,128)(2,1)} %near_hbm.1, s32[3,8]{1,0:T(4,128)} %bitcast.17, bf16[8,64,256]{2,1,0:T(8,128)(2,1)} %bitcast.14, bf16[8,64,256]{2,1,0:T(8,128)(2,1)} %bitcast.15, bf16[8,3,64,64]{3,2,1,0:T(8,128)(2,1)} %lcoup_hbm.1, ...), custom_call_target="tpu_custom_call" | custom-call | tf_op jit(solution)/shard_map/product/pallas_call | solution.py:527
  22.9 0.6 %copy.19 = bf16[8,256,16]{1,2,0:T(8,128)(2,1)} copy(bf16[8,256,16]{1,2,0:T(8,128)(2,1)S(1)} %bitcast.10) | data formatting | bytes 131072
